TPU v7x, 32 devices: a whole 2x2x4 slice. The times are simulated.
32 devices in a mesh: brick: 16 (over z, y, core), view: 2 (over x).
Axes of the slice: x: 2, y: 2, z: 4, core: 2. Of those that a mesh axis runs over, the one named last changes fastest.
Arguments:
- estimate: float32 [256, 128, 128], P('brick', 'view'), may hold values from 0.5 to 2
- views_data: float32 [2, 256, 128, 128], P('view', 'brick'), may hold values from 0.5 to 2
- psf_taps: float32 [2, 3, 17], P('view'), may hold values from 0.05 to 1
- view_offsets: int32 [2, 2], P('view'), may hold values from -4 to 4
- coverage: int32 [16, 2], P('brick'), may hold values from 0 to 1, as said below
Outputs:
- deconvolved: float32 [256, 128, 128], P('brick', 'view')
Inputs may be any that keep to these rules, and one draw needn't show every extreme that they name: `coverage`: every slab is covered by at least one view.
All inputs are finite; a program needn't handle non-finite values.
Results may differ from a plain program's by a relative error of at most 0.0001.
Values sent between devices are 32-bit elements; how exact they have to be, the bound alone decides.
No kernel may reach another device: no remote copies, remote signals or barrier semaphores. Data moves between devices by JAX's collectives and lax.ppermute only.
A program may use at most 64 MiB of HBM per device.

v0:
```python
import jax
import jax.numpy as jnp
from jax import lax
from jax.experimental import pallas as pl
from jax.experimental.pallas import tpu as pltpu
from jax.sharding import PartitionSpec as P


R = 8
ITERS = 4
HALO = 2 * R

F32, BF16 = jnp.float32, jnp.bfloat16
VMEM = pl.BlockSpec(memory_space=pltpu.VMEM)
SMEM = pl.BlockSpec(memory_space=pltpu.SMEM)
TAPS = 2 * R + 1


def parts(x):
    top = x.astype(BF16)
    return top, (x - top.astype(F32)).astype(BF16)


def dot(a, b):
    return jnp.dot(a, b, preferred_element_type=F32)


def stack3(blocks):
    split = [parts(b) for b in blocks]
    tops, rests = [s[0] for s in split], [s[1] for s in split]
    return jnp.concatenate(tops + rests + tops, axis=0)


class Piece:
    def __init__(self, array, rows, start=0):
        self.array, self.rows, self.start = array, rows, start

    def on(self, ref):
        return Piece(ref, self.rows, self.start)

    def layer(self, z):
        return self.array[pl.ds(self.start + z * self.rows, self.rows), :]

    def tile(self, z, y):
        return self.array[pl.ds(pl.multiple_of(self.start + z * self.rows + y, R), R), :]


def call(body, scalars, pieces, out_shape, scratch, vmem, cost):
    arrays = []
    for piece in pieces:
        if not any(piece.array is array for array in arrays):
            arrays.append(piece.array)
    where = [next(i for i, array in enumerate(arrays) if array is p.array) for p in pieces]

    def kernel(*refs):
        inputs = refs[len(scalars) : len(scalars) + len(arrays)]
        body(
            refs[: len(scalars)],
            [p.on(inputs[i]) for p, i in zip(pieces, where)],
            *refs[len(scalars) + len(arrays) :],
        )

    return pl.pallas_call(
        kernel,
        out_shape=out_shape,
        in_specs=[SMEM] * len(scalars) + [VMEM] * len(arrays),
        out_specs=[VMEM] * len(out_shape),
        scratch_shapes=scratch,
        compiler_params=pltpu.CompilerParams(vmem_limit_bytes=vmem << 20),
        cost_estimate=pl.CostEstimate(flops=cost, bytes_accessed=1 << 20, transcendentals=0),
    )(*scalars, *arrays)


def blur_rows_and_columns(depth, own, side, ly, bx, mid, out, flip):
    views, width = bx.shape[0], bx.shape[1] // 2
    window = own.rows + side.rows
    for z in range(0, depth, 2):
        pair = stack3(
            [jnp.concatenate([p.layer(z), p.layer(z + 1)], axis=1) for p in (own, side)]
        )
        result = dot(ly[...], pair)
        for v in range(views):
            for i in range(2):
                top, rest = parts(result[v * window : (v + 1) * window, i * width : (i + 1) * width])
                at = pl.ds((z + i) * window, window)
                mid[v, at, :width] = top
                mid[v, at, width:] = rest
    for v in range(views):
        for z in range(0, depth, 4):
            wide = dot(mid[v, pl.ds(z * window, 4 * window), :], bx[v])
            value = wide[:, :width] + wide[:, width:]
            for i in range(4):
                to = depth - 1 - z - i if flip else z + i
                out[v, to] = value[i * window : (i + 1) * window]


def ratios(seen, blurred):
    return [jnp.where(b > 0, d / b, 0.0) for d, b in zip(seen, blurred)]


def gather(total, at, term):
    total[at] = term if total[at] is None else total[at] + term


def near(depth, own, side, own_in, side_in, data_own, data_in, tables):
    taps, ly, bx = tables[:3]
    views, width = bx.shape[0], bx.shape[1] // 2
    window = own.rows + side.rows

    def body(_, pieces, blur_far, back, blur_own, blur_in, mid):
        own, side, own_in, side_in, taps, ly, bx = pieces[:7]
        taps, ly, bx = taps.array, ly.array, bx.array
        data_own, data_in = pieces[7 : 7 + views], pieces[7 + views :]
        blur_rows_and_columns(depth, own, side, ly, bx, mid, blur_own, False)
        blur_rows_and_columns(depth, own_in, side_in, ly, bx, mid, blur_in, True)
        for v in range(views):

            @pl.loop(0, window // R)
            def _(tile):
                y = pl.multiple_of(tile * R, R)
                at = pl.ds(y, R)
                load = lambda i: blur_own[v, i, at, :] if i < depth else blur_in[v, i - depth, at, :]
                blurred = [None] * depth
                for k in range(TAPS):
                    t = taps[v, k]
                    for j in range(depth):
                        gather(blurred, j, t * load(j + k))
                seen = [data_own[v].tile(j, y) for j in range(R)]
                seen += [data_in[v].tile(R - 1 - j, y) for j in range(R)]
                ratio = ratios(seen, blurred)
                total = [None] * depth
                for d in range(depth):
                    t = taps[v, d]
                    for j in range(depth - d):
                        gather(total, j + d, t * ratio[j])
                for z in range(depth):
                    back[v, z, at, :] = total[z]
                partial = [None] * depth
                for k in range(1, TAPS):
                    t = taps[v, k]
                    for j in range(depth - k, depth):
                        gather(partial, j, t * load(j + k - depth))
                for j in range(depth):
                    blur_far[v, j, at, :] = partial[j]

    shape = (views, depth, window, width)
    return call(
        body,
        [],
        [own, side, own_in, side_in] + [Piece(t, 0) for t in (taps, ly, bx)] + [*data_own, *data_in],
        [jax.ShapeDtypeStruct(shape, F32)] * 2,
        [pltpu.VMEM(shape, F32)] * 2 + [pltpu.VMEM((views, depth * window, 2 * width), BF16)],
        24 if views == 2 else 48,
        views * 10**9,
    )


def far(last, depth, scalars, est, own_out, side_out, blur_far, back, data_out, data_own, tables):
    views, width = tables[2].shape[0], tables[2].shape[1] // 2
    window, rows = own_out.rows + side_out.rows, est.rows

    def body(scalars, pieces, *refs):
        place, cover = scalars
        est, own_out, side_out = pieces[:3]
        blur_far, back, taps, ly, bx, lyt, bxt = [p.array for p in pieces[3:10]]
        data_out, data_own = pieces[10 : 10 + views], pieces[10 + views :]
        out, edge = refs[0], None if last else refs[1]
        blur_out, full, mid = refs[-3:]
        even = place[0] == 0
        blur_rows_and_columns(depth, own_out, side_out, ly, bx, mid, blur_out, True)
        for v in range(views):

            @pl.loop(0, window // R)
            def _(tile):
                y = pl.multiple_of(tile * R, R)
                at = pl.ds(y, R)
                blurred = [blur_far[v, j, at, :] for j in range(depth)]
                for k in range(depth):
                    t = taps[v, k]
                    for j in range(depth - k):
                        blurred[j] = blurred[j] + t * blur_out[v, j + k, at, :]
                seen = [data_out[v].tile(R - 1 - j, y) for j in range(R)]
                seen += [data_own[v].tile(j, y) for j in range(R)]
                ratio = ratios(seen, blurred)
                total = [back[v, z, at, :] for z in range(depth)]
                for d in range(depth):
                    t = taps[v, 2 * R - d]
                    for z in range(depth - d):
                        total[z] = total[z] + t * ratio[z + d]
                for z in range(depth):
                    full[v, z, at, :] = total[z]

        for z in range(0, depth, 2):
            for v in range(views):
                both = jnp.concatenate([full[v, z], full[v, z + 1]], axis=1)
                result = dot(lyt[v], stack3([both]))
                for i in range(2):
                    top, rest = parts(result[:, i * width : (i + 1) * width])
                    at = pl.ds((z + i) * rows, rows)
                    mid[v, at, :width] = top
                    mid[v, at, width:] = rest
        if views == 2:
            chosen = [cover[0, place[1]], cover[0, 1 - place[1]]]
        else:
            chosen = [cover[0, v] for v in range(views)]
        count = sum(chosen).astype(F32)
        for z in range(0, depth, 4):
            factor = None
            for v in range(views):
                wide = dot(mid[v, pl.ds(z * rows, 4 * rows), :], bxt[v])
                value = wide[:, :width] + wide[:, width:]
                if views == 2:
                    alone = chosen[1 - v] == 0
                    power = jnp.where(alone, value, jnp.sqrt(value))
                    power = jnp.where(chosen[v] == 0, 1.0, power)
                    factor = power if factor is None else factor * power
                else:
                    term = chosen[v].astype(F32) * jnp.log(value)
                    factor = term if factor is None else factor + term
            if views != 2:
                factor = jnp.exp(factor / count)
            for i in range(4):
                new = est.layer(z + i) * factor[i * rows : (i + 1) * rows]
                if last:
                    out[lax.select(even, jnp.int32(z + i), jnp.int32(depth - 1 - z - i))] = new
                else:
                    out[pl.ds((z + i) * rows, rows), :] = new
                    edge[pl.ds((z + i) * HALO, HALO), :] = jnp.where(
                        place[1] == 0, new[rows - HALO :], new[:HALO]
                    )

    shape = (views, depth, window, width)
    if last:
        outs = [jax.ShapeDtypeStruct((depth, rows, width), F32)]
    else:
        outs = [jax.ShapeDtypeStruct((depth * n, width), F32) for n in (rows, HALO)]
    return call(
        body,
        scalars,
        [est, own_out, side_out]
        + [Piece(t, 0) for t in (blur_far, back, *tables)]
        + [*data_out, *data_own],
        outs,
        [pltpu.VMEM(shape, F32)] * 2 + [pltpu.VMEM((views, depth * window, 2 * width), BF16)],
        24 if views == 2 else 48,
        views * 10**9,
    )


def normalized(taps):
    return taps / jnp.sum(taps, axis=-1, keepdims=True)


def small_rows(taps, first_shift, second_shift, width):
    lane = lax.broadcasted_iota(jnp.int32, (1, width), 1)
    shifts = jnp.where(lane == 0, first_shift.astype(F32), second_shift.astype(F32))
    return normalized(taps), shifts


def bands(place, smalls, rows, window, width):
    views, triple = len(smalls), 3 * window
    iota = lambda shape, dim: lax.broadcasted_iota(jnp.int32, shape, dim)

    def body(scalars, smalls, spread, ly, bx, lyt, bxt):
        (place,) = scalars
        low = place[2]

        def position(c):
            return jnp.where(c < rows, c, jnp.where(c < rows + low, c - rows - HALO, c - low))

        def split(value):
            top = value.astype(BF16).astype(F32)
            return top, value - top

        for v, piece in enumerate(smalls):
            small = piece.layer(0)

            def values(d, index):
                total = jnp.zeros(index.shape, F32)
                for k in range(TAPS):
                    total = jnp.where(index == k, small[d : d + 1, k : k + 1], total)
                return total

            shift = jnp.round(small[3:4, :]).astype(jnp.int32)
            for k in range(TAPS):
                there, back = small[0:1, k : k + 1], small[0:1, TAPS - 1 - k : TAPS - k]
                spread[v, k] = jnp.broadcast_to(jnp.where(place[0] == 0, there, back), (R, width))
            for out, height, mirror in ((ly, window, False), (lyt, rows, True)):
                col = iota((height, triple), 1)
                folded = position(
                    jnp.where(col < window, col, jnp.where(col < 2 * window, col - window, col - 2 * window))
                )
                line = position(iota((height, triple), 0))
                index = (line - folded if mirror else folded - line) + shift[:, 0:1] + R
                top, rest = split(values(1, index))
                both = jnp.where(col < 2 * window, top, rest).astype(BF16)
                if mirror:
                    out[v] = both
                else:
                    out[pl.ds(v * window, window), :] = both
            step = iota((width, width), 1) - iota((width, width), 0)
            for out, index in ((bx, -step), (bxt, step)):
                top, rest = split(values(2, index + shift[:, 1:2] + R))
                for i in range(2):
                    at = pl.ds(i * width, width)
                    out[v, at, :width] = top.astype(BF16)
                    out[v, at, width:] = rest.astype(BF16)

    shapes = [
        (views * window, triple),
        (views, 2 * width, 2 * width),
        (views, rows, triple),
        (views, 2 * width, 2 * width),
    ]
    return call(
        body,
        [place],
        smalls,
        [jax.ShapeDtypeStruct((views, TAPS, R, width), F32)]
        + [jax.ShapeDtypeStruct(s, BF16) for s in shapes],
        [],
        8,
        views * 10**8,
    )


def prepare(place, estimate, views_data, psf_taps, view_offsets):
    depth, rows, width = estimate.shape
    total = views_data.shape[2]
    window, half = rows + HALO, depth // 2

    def body(place, offsets, estimate, recorded, psf, outer, inner, across, corner, beside):
        mine, theirs = place[1], 1 - place[1]
        edge = pl.multiple_of(jnp.where(mine == 0, rows - HALO, 0), HALO)
        taps, shifts = small_rows(psf[0], offsets[0, 0], offsets[0, 1], width)
        small = depth * HALO + half * window
        across[pl.ds(small, R), :] = jnp.zeros((R, width), F32)
        across[pl.ds(small, 3), :TAPS] = taps
        across[pl.ds(small + 3, 1), :] = shifts

        def window_rows(view, at, out, to):
            start = pl.multiple_of(view * rows, R)
            out[pl.ds(to, rows), :] = recorded[0, at, pl.ds(start, rows), :]
            start = pl.multiple_of(jnp.where(view == 0, rows, total - rows - HALO), R)
            out[pl.ds(to + rows, HALO), :] = recorded[0, at, pl.ds(start, HALO), :]

        for z in range(depth):
            at = lax.select(place[0] == 0, jnp.int32(z), jnp.int32(depth - 1 - z))
            layer, strip = estimate[at], estimate[at, pl.ds(edge, HALO), :]
            for out in (outer, inner):
                out[pl.ds(z * rows, rows), :] = layer
            for out in (across, corner):
                out[pl.ds(z * HALO, HALO), :] = strip
            if z < half:
                window_rows(mine, at, outer, depth * rows + z * window)
                window_rows(theirs, at, corner, depth * HALO + z * window)
                window_rows(theirs, at, beside, z * window)
            else:
                window_rows(mine, at, inner, depth * rows + (z - half) * window)
                window_rows(theirs, at, across, depth * HALO + (z - half) * window)

    heights = [
        depth * rows + half * window,
        depth * rows + half * window,
        depth * HALO + half * window + R,
        depth * HALO + half * window,
        half * window,
    ]
    return pl.pallas_call(
        body,
        out_shape=[jax.ShapeDtypeStruct((height, width), F32) for height in heights],
        in_specs=[SMEM] * 2 + [VMEM] * 3,
        out_specs=[VMEM] * 5,
        compiler_params=pltpu.CompilerParams(vmem_limit_bytes=10 << 20),
        cost_estimate=pl.CostEstimate(flops=0, bytes_accessed=8 << 20, transcendentals=0),
        name="prepare",
    )(place, view_offsets, estimate, views_data, psf_taps)


def pair_lists(count):
    inner = [(i, i + 1) for i in range(0, count - 1, 2)]
    outer = [(i, i + 1) for i in range(1, count - 1, 2)]
    both = lambda pairs: [p for a, b in pairs for p in ((a, b), (b, a))]
    return both(inner), both(outer)


def diagonal(pairs):
    return [(2 * a + v, 2 * b + 1 - v) for a, b in pairs for v in range(2)]


def two_view_plan(estimate, views_data, psf_taps, view_offsets, place, inner, outer):
    swap = [(0, 1), (1, 0)]
    depth, rows, _ = estimate.shape
    window = rows + HALO
    both = ("brick", "view")
    wide, thin = depth * rows, depth * HALO
    small = thin + depth // 2 * window

    def halo(current, edge):
        if edge is None:
            return start
        outer_z = lax.ppermute(current.array, "brick", outer)
        side = lax.ppermute(edge, "view", swap)
        inner_z = lax.ppermute(current.array, "brick", inner)
        outer_side = lax.ppermute(edge, both, diagonal(outer))
        inner_side = lax.ppermute(side, "brick", inner)
        return (
            Piece(side, HALO), Piece(inner_z, rows), Piece(inner_side, HALO),
            Piece(outer_z, rows), Piece(outer_side, HALO),
        )

    to_outer, to_inner, across, corner, beside = prepare(
        place, estimate, views_data, psf_taps, view_offsets
    )
    from_outer = lax.ppermute(to_outer, "brick", outer)
    from_side = lax.ppermute(across, "view", swap)
    from_inner = lax.ppermute(to_inner, "brick", inner)
    from_corner = lax.ppermute(corner, both, diagonal(outer))
    from_beside = lax.ppermute(beside, "view", swap)
    from_inner_side = lax.ppermute(from_side, "brick", inner)
    start = (
        Piece(from_side, HALO), Piece(from_inner, rows), Piece(from_inner_side, HALO),
        Piece(from_outer, rows), Piece(from_corner, HALO),
    )
    near_data = (
        (Piece(to_inner, window, wide), Piece(from_side, window, thin)),
        (Piece(from_inner, window, wide), Piece(from_inner_side, window, thin)),
    )
    far_data = (
        (Piece(from_outer, window, wide), Piece(from_corner, window, thin)),
        (Piece(to_outer, window, wide), Piece(from_beside, window)),
    )
    smalls = (Piece(across, R, small), Piece(from_side, R, small))
    return Piece(to_inner, rows), smalls, near_data, far_data, halo, window


def many_view_plan(estimate, views_data, psf_taps, view_offsets, place, inner, outer):
    depth, rows, width = estimate.shape
    even = place[0] == 0
    up = [(i, i + 1) for i in range(lax.axis_size("view") - 1)]
    down = [(b, a) for a, b in up]
    flat = lambda array: Piece(array.reshape(-1, width), array.shape[1])

    def beside(block, dim):
        low = lax.slice_in_dim(block, rows - HALO, rows, axis=dim)
        high = lax.slice_in_dim(block, 0, HALO, axis=dim)
        return jnp.concatenate(
            [lax.ppermute(low, "view", up), lax.ppermute(high, "view", down)], axis=dim
        )

    def halo(current, _):
        block = current.array.reshape(depth, rows, width)
        inner_z = lax.ppermute(block, "brick", inner)
        outer_z = lax.ppermute(block, "brick", outer)
        pieces = beside(block, 1), inner_z, beside(inner_z, 1), outer_z, beside(outer_z, 1)
        return tuple(flat(piece) for piece in pieces)

    taps, shifts = small_rows(psf_taps[0], view_offsets[0, 0], view_offsets[0, 1], width)
    taps = jnp.pad(taps, ((0, 0), (0, width - TAPS)))
    small = jnp.concatenate([taps, shifts, jnp.zeros((R - 4, width), F32)])
    smalls = lax.all_gather(small, "view", axis=0, tiled=True)
    data = lax.all_to_all(views_data, "view", split_axis=2, concat_axis=0, tiled=True)
    data = jnp.where(even, data, data[:, ::-1])
    data = jnp.concatenate([data, beside(data, 2)], axis=2)
    views = range(data.shape[0])
    ends = lambda array: tuple(flat(array[v]) for v in views)
    mine_in, mine_out = data[:, -R:], data[:, :R]
    near_data = ends(mine_in), ends(lax.ppermute(mine_in, "brick", inner))
    far_data = ends(lax.ppermute(mine_out, "brick", outer)), ends(mine_out)
    current = flat(jnp.where(even, estimate, estimate[::-1]))
    smalls = tuple(Piece(smalls, R, v * R) for v in views)
    return current, smalls, near_data, far_data, halo, rows + 2 * HALO


def shards(estimate, views_data, psf_taps, view_offsets, coverage):
    brick, view = lax.axis_index("brick"), lax.axis_index("view")
    depth, rows, width = estimate.shape
    inner, outer = pair_lists(lax.axis_size("brick"))
    pair = lax.axis_size("view") == 2
    plan = two_view_plan if pair else many_view_plan
    low = jnp.where(view == 0, 0, HALO) if pair else HALO
    place = jnp.stack([lax.rem(brick, 2), view, low]).astype(jnp.int32)
    current, smalls, near_data, far_data, halo, window = plan(
        estimate, views_data, psf_taps, view_offsets, place, inner, outer
    )
    tables = bands(place, smalls, rows, window, width)
    edge = None
    for step in range(ITERS):
        last = step == ITERS - 1
        side, inner_z, inner_side, outer_z, outer_side = halo(current, edge)
        blur_far, back = near(
            depth, current, side, inner_z, inner_side, *near_data, tables
        )
        results = far(
            last, depth, [place, coverage], current, outer_z, outer_side,
            blur_far, back, *far_data, tables,
        )
        if not last:
            current, edge = Piece(results[0], rows), results[1]
    return results[0]


def solution(mesh):
    return jax.shard_map(
        shards,
        mesh=mesh,
        in_specs=(
            P("brick", "view", None),
            P("view", "brick", None, None),
            P("view", None, None),
            P("view", None),
            P("brick", None),
        ),
        out_specs=P("brick", "view", None),
        check_vma=False,
    )
```

profile of v0, /device:TPU:17, one launch (start us, length us, event | category | flops | bytes accessed | tf_op | source)
XLA Modules:
  0.0 113.3 jit_solution(10237935323501508483)
XLA Ops:
  0.0 0.7 copy.6.psf
  0.7 0.1 pad_add_fusion.place.refs_0_
  0.8 1.2 %copy-done = f32[1,16,128,128]{3,2,1,0:T(8,128)S(1)} copy-done((f32[1,16,128,128]{3,2,1,0:T(8,128)S(1)}, f32[1,16,128,128]{3,2,1,0:T(8,128)}, u32[]{:S(2)}) %copy-start) | copy-done | bytes 1048600
  2.0 1.0 copy-done.1
  3.0 0.7 copy-done.2
  3.7 0.7 prepare.1
  4.4 1.3 %collective-permute-start.2 = (f32[904,128]{1,0:T(8,128)S(1)}, f32[904,128]{1,0:T(8,128)S(1)}, u32[]{:S(2)}, u32[]{:S(2)}) collective-permute-start(f32[904,128]{1,0:T(8,128)S(1)} %get-tuple-element.32.refs_1_), channel_id=1, source_target_pairs={{0,1},{1,0},{2,3},{3,2},{4,5},{5,4},{6,7},{7,6},{8,9},{9,8},{10,11... | collective-permute-start | bytes 1388552 | tf_op jit(solution)/shard_map/ppermute | solution.py:416
  5.7 1.0 collective-permute-start.3
  6.7 3.0 %collective-permute-start = (f32[1664,128]{1,0:T(8,128)S(1)}, f32[1664,128]{1,0:T(8,128)S(1)}, u32[]{:S(2)}, u32[]{:S(2)}) collective-permute-start(f32[1664,128]{1,0:T(8,128)S(1)} %get-tuple-element.30.refs_12_.refs_14_), channel_id=1, source_target_pairs={{2,4},{4,2},{6,8},{8,6},{10,12},{12,10},{14,16},{16,14},{18,20},{2... | collective-permute-start | bytes 2555912 | tf_op jit(solution)/shard_map/ppermute | solution.py:415
  9.7 6.3 %collective-permute-done.2.refs_2_.refs_1_.refs_8_ = f32[904,128]{1,0:T(8,128)S(1)} collective-permute-done((f32[904,128]{1,0:T(8,128)S(1)}, f32[904,128]{1,0:T(8,128)S(1)}, u32[]{:S(2)}, u32[]{:S(2)}) %collective-permute-start.2) | collective-permute-done | bytes 462880 | tf_op jit(solution)/shard_map/ppermute | solution.py:416
  16.0 1.5 %collective-permute-start.4 = (f32[904,128]{1,0:T(8,128)S(1)}, f32[904,128]{1,0:T(8,128)S(1)}, u32[]{:S(2)}, u32[]{:S(2)}) collective-permute-start(f32[904,128]{1,0:T(8,128)S(1)} %collective-permute-done.2.refs_2_.refs_1_.refs_8_), channel_id=1, source_target_pairs={{0,2},{2,0},{4,6},{6,4},{8,10},{10,8},{12,14},{14,12},{16,18},{18,... | collective-permute-start | bytes 1388552 | tf_op jit(solution)/shard_map/ppermute | solution.py:420
  17.5 4.0 %collective-permute-start.1 = (f32[896,128]{1,0:T(8,128)S(1)}, f32[896,128]{1,0:T(8,128)S(1)}, u32[]{:S(2)}, u32[]{:S(2)}) collective-permute-start(f32[896,128]{1,0:T(8,128)S(1)} %get-tuple-element.31), channel_id=1, source_target_pairs={{2,5},{3,4},{4,3},{5,2},{6,9},{7,8},{8,7},{9,6},{10,13},{11,12},{1... | collective-permute-start | bytes 1376264 | tf_op jit(solution)/shard_map/ppermute | solution.py:418
  21.5 0.3 collective-permute-start.5
  21.8 2.2 %shard_map.55 = (f32[2,17,8,128]{3,2,1,0:T(8,128)S(1)}, bf16[160,240]{1,0:T(8,128)(2,1)S(1)}, bf16[2,256,256]{2,1,0:T(8,128)(2,1)S(1)}, bf16[2,64,240]{2,1,0:T(8,128)(2,1)S(1)}, bf16[2,256,256]{2,1,0:T(8,128)(2,1)S(1)}) custom-call(s32[3]{0:T(128)S(1)} %pad_add_fusion.place.refs_0_, f32[904,128]{1,0:T(8,128)S(1)} %get-tuple-element.32.refs_1_, ...), custom_call_target="tpu_custom_call" | custom-call | flops 200000000 | bytes 1048576 | tf_op jit(solution)/shard_map/pallas_call | solution.py:63
  24.1 4.7 %shard_map.56 = (f32[2,16,80,128]{3,2,1,0:T(8,128)S(1)}, f32[2,16,80,128]{3,2,1,0:T(8,128)S(1)}) custom-call(f32[1664,128]{1,0:T(8,128)S(1)} %get-tuple-element.29.refs_0_.refs_2_.refs_7_, f32[904,128]{1,0:T(8,128)S(1)} %collective-permute-done.2.refs_2_.refs_1_.refs_8_, f32[1664,128]{1,0:T(8,128)S(1)} %collective-permute-done.3.refs_2_.refs_9_, ...), custom_call_target="tpu_custom_call" | custom-call | flops 2000000000 | bytes 1048576 | tf_op jit(solution)/shard_map/pallas_call | solution.py:63
  28.8 10.8 %collective-permute-done.5.refs_13_.refs_15_ = f32[640,128]{1,0:T(8,128)S(1)} collective-permute-done((f32[640,128]{1,0:T(8,128)S(1)}, f32[640,128]{1,0:T(8,128)S(1)}, u32[]{:S(2)}, u32[]{:S(2)}) %collective-permute-start.5) | collective-permute-done | bytes 327712 | tf_op jit(solution)/shard_map/ppermute | solution.py:419
  39.6 0.1 collective-permute-done.refs_3_.refs_12_
  39.6 4.0 %shard_map.57 = (f32[1024,128]{1,0:T(8,128)S(1)}, f32[256,128]{1,0:T(8,128)S(1)}) custom-call(s32[3]{0:T(128)S(1)} %pad_add_fusion.place.refs_0_, s32[1,2]{1,0:T(1,128)S(1)} %copy-done.3, f32[1664,128]{1,0:T(8,128)S(1)} %get-tuple-element.29.refs_0_.refs_2_.refs_7_, f32[1664,128]{1,0:T(8,128)S(1)} %collective-permute-done.refs_3_.refs_12_, ...), custom_call_target="tpu_custom_call" | custom-call | flops 2000000000 | bytes 1048576 | tf_op jit(solution)/shard_map/pallas_call | solution.py:63
  43.6 0.1 collective-permute-start.9
  43.7 3.3 %collective-permute-start.6 = (f32[1024,128]{1,0:T(8,128)S(1)}, f32[1024,128]{1,0:T(8,128)S(1)}, u32[]{:S(2)}, u32[]{:S(2)}) collective-permute-start(f32[1024,128]{1,0:T(8,128)S(1)} %get-tuple-element.41.refs_0_.refs_2_), channel_id=1, source_target_pairs={{2,4},{4,2},{6,8},{8,6},{10,12},{12,10},{14,16},{16,14},{18,20},{2... | collective-permute-start | bytes 1572872 | tf_op jit(solution)/shard_map/ppermute | solution.py:402
  47.0 1.3 %collective-permute-start.8 = (f32[256,128]{1,0:T(8,128)S(1)}, f32[256,128]{1,0:T(8,128)S(1)}, u32[]{:S(2)}, u32[]{:S(2)}) collective-permute-start(f32[256,128]{1,0:T(8,128)S(1)} %get-tuple-element.42), channel_id=1, source_target_pairs={{0,1},{1,0},{2,3},{3,2},{4,5},{5,4},{6,7},{7,6},{8,9},{9,8},{10,11... | collective-permute-start | bytes 393224 | tf_op jit(solution)/shard_map/ppermute | solution.py:403
  48.3 3.5 %collective-permute-done.8.refs_1_ = f32[256,128]{1,0:T(8,128)S(1)} collective-permute-done((f32[256,128]{1,0:T(8,128)S(1)}, f32[256,128]{1,0:T(8,128)S(1)}, u32[]{:S(2)}, u32[]{:S(2)}) %collective-permute-start.8) | collective-permute-done | bytes 131104 | tf_op jit(solution)/shard_map/ppermute | solution.py:403
  51.8 1.2 %collective-permute-start.10 = (f32[256,128]{1,0:T(8,128)S(1)}, f32[256,128]{1,0:T(8,128)S(1)}, u32[]{:S(2)}, u32[]{:S(2)}) collective-permute-start(f32[256,128]{1,0:T(8,128)S(1)} %collective-permute-done.8.refs_1_), channel_id=1, source_target_pairs={{0,2},{2,0},{4,6},{6,4},{8,10},{10,8},{12,14},{14,12},{16,18},{18,... | collective-permute-start | bytes 393224 | tf_op jit(solution)/shard_map/ppermute | solution.py:406
  53.0 3.2 %collective-permute-start.7 = (f32[256,128]{1,0:T(8,128)S(1)}, f32[256,128]{1,0:T(8,128)S(1)}, u32[]{:S(2)}, u32[]{:S(2)}) collective-permute-start(f32[256,128]{1,0:T(8,128)S(1)} %get-tuple-element.42), channel_id=1, source_target_pairs={{2,5},{3,4},{4,3},{5,2},{6,9},{7,8},{8,7},{9,6},{10,13},{11,12},{1... | collective-permute-start | bytes 393224 | tf_op jit(solution)/shard_map/ppermute | solution.py:405
  56.2 4.7 %shard_map.58 = (f32[2,16,80,128]{3,2,1,0:T(8,128)S(1)}, f32[2,16,80,128]{3,2,1,0:T(8,128)S(1)}) custom-call(f32[1024,128]{1,0:T(8,128)S(1)} %get-tuple-element.41.refs_0_.refs_2_, f32[256,128]{1,0:T(8,128)S(1)} %collective-permute-done.8.refs_1_, f32[1024,128]{1,0:T(8,128)S(1)} %collective-permute-done.9.refs_2_, ...), custom_call_target="tpu_custom_call" | custom-call | flops 2000000000 | bytes 1048576 | tf_op jit(solution)/shard_map/pallas_call | solution.py:63
  60.9 0.8 collective-permute-done.7.refs_4_
  61.7 0.9 collective-permute-done.6.refs_3_
  62.6 4.0 %shard_map.59 = (f32[1024,128]{1,0:T(8,128)S(1)}, f32[256,128]{1,0:T(8,128)S(1)}) custom-call(s32[3]{0:T(128)S(1)} %pad_add_fusion.place.refs_0_, s32[1,2]{1,0:T(1,128)S(1)} %copy-done.3, f32[1024,128]{1,0:T(8,128)S(1)} %get-tuple-element.41.refs_0_.refs_2_, f32[1024,128]{1,0:T(8,128)S(1)} %collective-permute-done.6.refs_3_, ...), custom_call_target="tpu_custom_call" | custom-call | flops 2000000000 | bytes 1048576 | tf_op jit(solution)/shard_map/pallas_call | solution.py:63
  66.6 0.1 collective-permute-start.14
  66.6 3.3 %collective-permute-start.11 = (f32[1024,128]{1,0:T(8,128)S(1)}, f32[1024,128]{1,0:T(8,128)S(1)}, u32[]{:S(2)}, u32[]{:S(2)}) collective-permute-start(f32[1024,128]{1,0:T(8,128)S(1)} %get-tuple-element.45.refs_0_.refs_2_), channel_id=1, source_target_pairs={{2,4},{4,2},{6,8},{8,6},{10,12},{12,10},{14,16},{16,14},{18,20},{2... | collective-permute-start | bytes 1572872 | tf_op jit(solution)/shard_map/ppermute | solution.py:402
  70.0 1.3 %collective-permute-start.13 = (f32[256,128]{1,0:T(8,128)S(1)}, f32[256,128]{1,0:T(8,128)S(1)}, u32[]{:S(2)}, u32[]{:S(2)}) collective-permute-start(f32[256,128]{1,0:T(8,128)S(1)} %get-tuple-element.46), channel_id=1, source_target_pairs={{0,1},{1,0},{2,3},{3,2},{4,5},{5,4},{6,7},{7,6},{8,9},{9,8},{10,11... | collective-permute-start | bytes 393224 | tf_op jit(solution)/shard_map/ppermute | solution.py:403
  71.2 3.5 %collective-permute-done.13.refs_1_ = f32[256,128]{1,0:T(8,128)S(1)} collective-permute-done((f32[256,128]{1,0:T(8,128)S(1)}, f32[256,128]{1,0:T(8,128)S(1)}, u32[]{:S(2)}, u32[]{:S(2)}) %collective-permute-start.13) | collective-permute-done | bytes 131104 | tf_op jit(solution)/shard_map/ppermute | solution.py:403
  74.8 1.2 %collective-permute-start.15 = (f32[256,128]{1,0:T(8,128)S(1)}, f32[256,128]{1,0:T(8,128)S(1)}, u32[]{:S(2)}, u32[]{:S(2)}) collective-permute-start(f32[256,128]{1,0:T(8,128)S(1)} %collective-permute-done.13.refs_1_), channel_id=1, source_target_pairs={{0,2},{2,0},{4,6},{6,4},{8,10},{10,8},{12,14},{14,12},{16,18},{18,... | collective-permute-start | bytes 393224 | tf_op jit(solution)/shard_map/ppermute | solution.py:406
  76.0 3.3 %collective-permute-start.12 = (f32[256,128]{1,0:T(8,128)S(1)}, f32[256,128]{1,0:T(8,128)S(1)}, u32[]{:S(2)}, u32[]{:S(2)}) collective-permute-start(f32[256,128]{1,0:T(8,128)S(1)} %get-tuple-element.46), channel_id=1, source_target_pairs={{2,5},{3,4},{4,3},{5,2},{6,9},{7,8},{8,7},{9,6},{10,13},{11,12},{1... | collective-permute-start | bytes 393224 | tf_op jit(solution)/shard_map/ppermute | solution.py:405
  79.3 4.7 %shard_map.60 = (f32[2,16,80,128]{3,2,1,0:T(8,128)S(1)}, f32[2,16,80,128]{3,2,1,0:T(8,128)S(1)}) custom-call(f32[1024,128]{1,0:T(8,128)S(1)} %get-tuple-element.45.refs_0_.refs_2_, f32[256,128]{1,0:T(8,128)S(1)} %collective-permute-done.13.refs_1_, f32[1024,128]{1,0:T(8,128)S(1)} %collective-permute-done.14.refs_2_, ...), custom_call_target="tpu_custom_call" | custom-call | flops 2000000000 | bytes 1048576 | tf_op jit(solution)/shard_map/pallas_call | solution.py:63
  84.0 0.6 collective-permute-done.12.refs_4_
  84.6 0.9 collective-permute-done.11.refs_3_
  85.6 4.0 %shard_map.61 = (f32[1024,128]{1,0:T(8,128)S(1)}, f32[256,128]{1,0:T(8,128)S(1)}) custom-call(s32[3]{0:T(128)S(1)} %pad_add_fusion.place.refs_0_, s32[1,2]{1,0:T(1,128)S(1)} %copy-done.3, f32[1024,128]{1,0:T(8,128)S(1)} %get-tuple-element.45.refs_0_.refs_2_, f32[1024,128]{1,0:T(8,128)S(1)} %collective-permute-done.11.refs_3_, ...), custom_call_target="tpu_custom_call" | custom-call | flops 2000000000 | bytes 1048576 | tf_op jit(solution)/shard_map/pallas_call | solution.py:63
  89.5 0.1 collective-permute-start.19
  89.6 3.3 %collective-permute-start.16 = (f32[1024,128]{1,0:T(8,128)S(1)}, f32[1024,128]{1,0:T(8,128)S(1)}, u32[]{:S(2)}, u32[]{:S(2)}) collective-permute-start(f32[1024,128]{1,0:T(8,128)S(1)} %get-tuple-element.49.refs_0_.refs_2_), channel_id=1, source_target_pairs={{2,4},{4,2},{6,8},{8,6},{10,12},{12,10},{14,16},{16,14},{18,20},{2... | collective-permute-start | bytes 1572872 | tf_op jit(solution)/shard_map/ppermute | solution.py:402
  93.0 1.3 %collective-permute-start.18 = (f32[256,128]{1,0:T(8,128)S(1)}, f32[256,128]{1,0:T(8,128)S(1)}, u32[]{:S(2)}, u32[]{:S(2)}) collective-permute-start(f32[256,128]{1,0:T(8,128)S(1)} %get-tuple-element.50), channel_id=1, source_target_pairs={{0,1},{1,0},{2,3},{3,2},{4,5},{5,4},{6,7},{7,6},{8,9},{9,8},{10,11... | collective-permute-start | bytes 393224 | tf_op jit(solution)/shard_map/ppermute | solution.py:403
  94.2 3.5 %collective-permute-done.18.refs_1_ = f32[256,128]{1,0:T(8,128)S(1)} collective-permute-done((f32[256,128]{1,0:T(8,128)S(1)}, f32[256,128]{1,0:T(8,128)S(1)}, u32[]{:S(2)}, u32[]{:S(2)}) %collective-permute-start.18) | collective-permute-done | bytes 131104 | tf_op jit(solution)/shard_map/ppermute | solution.py:403
  97.7 1.2 %collective-permute-start.20 = (f32[256,128]{1,0:T(8,128)S(1)}, f32[256,128]{1,0:T(8,128)S(1)}, u32[]{:S(2)}, u32[]{:S(2)}) collective-permute-start(f32[256,128]{1,0:T(8,128)S(1)} %collective-permute-done.18.refs_1_), channel_id=1, source_target_pairs={{0,2},{2,0},{4,6},{6,4},{8,10},{10,8},{12,14},{14,12},{16,18},{18,... | collective-permute-start | bytes 393224 | tf_op jit(solution)/shard_map/ppermute | solution.py:406
  98.9 3.2 %collective-permute-start.17 = (f32[256,128]{1,0:T(8,128)S(1)}, f32[256,128]{1,0:T(8,128)S(1)}, u32[]{:S(2)}, u32[]{:S(2)}) collective-permute-start(f32[256,128]{1,0:T(8,128)S(1)} %get-tuple-element.50), channel_id=1, source_target_pairs={{2,5},{3,4},{4,3},{5,2},{6,9},{7,8},{8,7},{9,6},{10,13},{11,12},{1... | collective-permute-start | bytes 393224 | tf_op jit(solution)/shard_map/ppermute | solution.py:405
  102.1 4.7 %shard_map.62 = (f32[2,16,80,128]{3,2,1,0:T(8,128)S(1)}, f32[2,16,80,128]{3,2,1,0:T(8,128)S(1)}) custom-call(f32[1024,128]{1,0:T(8,128)S(1)} %get-tuple-element.49.refs_0_.refs_2_, f32[256,128]{1,0:T(8,128)S(1)} %collective-permute-done.18.refs_1_, f32[1024,128]{1,0:T(8,128)S(1)} %collective-permute-done.19.refs_2_, ...), custom_call_target="tpu_custom_call" | custom-call | flops 2000000000 | bytes 1048576 | tf_op jit(solution)/shard_map/pallas_call | solution.py:63
  106.8 0.8 collective-permute-done.17.refs_4_
  107.6 0.9 collective-permute-done.16.refs_3_
  108.5 4.7 %shard_map.63 = f32[16,64,128]{2,1,0:T(8,128)} custom-call(s32[3]{0:T(128)S(1)} %pad_add_fusion.place.refs_0_, s32[1,2]{1,0:T(1,128)S(1)} %copy-done.3, f32[1024,128]{1,0:T(8,128)S(1)} %get-tuple-element.49.refs_0_.refs_2_, f32[1024,128]{1,0:T(8,128)S(1)} %collective-permute-done.16.refs_3_, f32[256,128]{1,0:T(8,128)S(1)} %collective-permute-done.17.refs_4_, ...), custom_call_target="tpu_custom_call" | custom-call | flops 2000000000 | bytes 1048576 | tf_op jit(solution)/shard_map/pallas_call | solution.py:63
  (14 shorter events, 0.0 us)
Async XLA Ops:
  0.8 1.2 %copy-start = (f32[1,16,128,128]{3,2,1,0:T(8,128)S(1)}, f32[1,16,128,128]{3,2,1,0:T(8,128)}, u32[]{:S(2)}) copy-start(f32[1,16,128,128]{3,2,1,0:T(8,128)} %recorded.1) | copy-start | bytes 3145732
  2.0 1.0 copy-start.1
  3.0 0.7 copy-start.2
  4.4 11.6 %collective-permute-start.2 = (f32[904,128]{1,0:T(8,128)S(1)}, f32[904,128]{1,0:T(8,128)S(1)}, u32[]{:S(2)}, u32[]{:S(2)}) collective-permute-start(f32[904,128]{1,0:T(8,128)S(1)} %get-tuple-element.32.refs_1_), channel_id=1, source_target_pairs={{0,1},{1,0},{2,3},{3,2},{4,5},{5,4},{6,7},{7,6},{8,9},{9,8},{10,11... | collective-permute-start | bytes 1388552 | tf_op jit(solution)/shard_map/ppermute | solution.py:416
  5.7 18.3 %collective-permute-start.3 = (f32[1664,128]{1,0:T(8,128)S(1)}, f32[1664,128]{1,0:T(8,128)S(1)}, u32[]{:S(2)}, u32[]{:S(2)}) collective-permute-start(f32[1664,128]{1,0:T(8,128)S(1)} %get-tuple-element.29.refs_0_.refs_2_.refs_7_), channel_id=1, source_target_pairs={{0,2},{2,0},{4,6},{6,4},{8,10},{10,8},{12,14},{14,12},{16,18},{18,... | collective-permute-start | bytes 2555912 | tf_op jit(solution)/shard_map/ppermute | solution.py:417
  6.7 33.0 %collective-permute-start = (f32[1664,128]{1,0:T(8,128)S(1)}, f32[1664,128]{1,0:T(8,128)S(1)}, u32[]{:S(2)}, u32[]{:S(2)}) collective-permute-start(f32[1664,128]{1,0:T(8,128)S(1)} %get-tuple-element.30.refs_12_.refs_14_), channel_id=1, source_target_pairs={{2,4},{4,2},{6,8},{8,6},{10,12},{12,10},{14,16},{16,14},{18,20},{2... | collective-permute-start | bytes 2555912 | tf_op jit(solution)/shard_map/ppermute | solution.py:415
  16.0 8.1 %collective-permute-start.4 = (f32[904,128]{1,0:T(8,128)S(1)}, f32[904,128]{1,0:T(8,128)S(1)}, u32[]{:S(2)}, u32[]{:S(2)}) collective-permute-start(f32[904,128]{1,0:T(8,128)S(1)} %collective-permute-done.2.refs_2_.refs_1_.refs_8_), channel_id=1, source_target_pairs={{0,2},{2,0},{4,6},{6,4},{8,10},{10,8},{12,14},{14,12},{16,18},{18,... | collective-permute-start | bytes 1388552 | tf_op jit(solution)/shard_map/ppermute | solution.py:420
  17.5 22.0 %collective-permute-start.1 = (f32[896,128]{1,0:T(8,128)S(1)}, f32[896,128]{1,0:T(8,128)S(1)}, u32[]{:S(2)}, u32[]{:S(2)}) collective-permute-start(f32[896,128]{1,0:T(8,128)S(1)} %get-tuple-element.31), channel_id=1, source_target_pairs={{2,5},{3,4},{4,3},{5,2},{6,9},{7,8},{8,7},{9,6},{10,13},{11,12},{1... | collective-permute-start | bytes 1376264 | tf_op jit(solution)/shard_map/ppermute | solution.py:418
  21.5 18.1 %collective-permute-start.5 = (f32[640,128]{1,0:T(8,128)S(1)}, f32[640,128]{1,0:T(8,128)S(1)}, u32[]{:S(2)}, u32[]{:S(2)}) collective-permute-start(f32[640,128]{1,0:T(8,128)S(1)} %get-tuple-element.40), channel_id=1, source_target_pairs={{0,1},{1,0},{2,3},{3,2},{4,5},{5,4},{6,7},{7,6},{8,9},{9,8},{10,11... | collective-permute-start | bytes 983048 | tf_op jit(solution)/shard_map/ppermute | solution.py:419
  24.1 15.6 %copy-start.3 = (s32[1,2]{1,0:T(1,128)S(1)}, s32[1,2]{1,0:T(1,128)}, u32[]{:S(2)}) copy-start(s32[1,2]{1,0:T(1,128)} %refs_1_.7) | copy-start | bytes 28
  43.6 12.6 %collective-permute-start.9 = (f32[1024,128]{1,0:T(8,128)S(1)}, f32[1024,128]{1,0:T(8,128)S(1)}, u32[]{:S(2)}, u32[]{:S(2)}) collective-permute-start(f32[1024,128]{1,0:T(8,128)S(1)} %get-tuple-element.41.refs_0_.refs_2_), channel_id=1, source_target_pairs={{0,2},{2,0},{4,6},{6,4},{8,10},{10,8},{12,14},{14,12},{16,18},{18,... | collective-permute-start | bytes 1572872 | tf_op jit(solution)/shard_map/ppermute | solution.py:404
  43.7 18.9 %collective-permute-start.6 = (f32[1024,128]{1,0:T(8,128)S(1)}, f32[1024,128]{1,0:T(8,128)S(1)}, u32[]{:S(2)}, u32[]{:S(2)}) collective-permute-start(f32[1024,128]{1,0:T(8,128)S(1)} %get-tuple-element.41.refs_0_.refs_2_), channel_id=1, source_target_pairs={{2,4},{4,2},{6,8},{8,6},{10,12},{12,10},{14,16},{16,14},{18,20},{2... | collective-permute-start | bytes 1572872 | tf_op jit(solution)/shard_map/ppermute | solution.py:402
  47.0 4.8 %collective-permute-start.8 = (f32[256,128]{1,0:T(8,128)S(1)}, f32[256,128]{1,0:T(8,128)S(1)}, u32[]{:S(2)}, u32[]{:S(2)}) collective-permute-start(f32[256,128]{1,0:T(8,128)S(1)} %get-tuple-element.42), channel_id=1, source_target_pairs={{0,1},{1,0},{2,3},{3,2},{4,5},{5,4},{6,7},{7,6},{8,9},{9,8},{10,11... | collective-permute-start | bytes 393224 | tf_op jit(solution)/shard_map/ppermute | solution.py:403
  51.8 4.4 %collective-permute-start.10 = (f32[256,128]{1,0:T(8,128)S(1)}, f32[256,128]{1,0:T(8,128)S(1)}, u32[]{:S(2)}, u32[]{:S(2)}) collective-permute-start(f32[256,128]{1,0:T(8,128)S(1)} %collective-permute-done.8.refs_1_), channel_id=1, source_target_pairs={{0,2},{2,0},{4,6},{6,4},{8,10},{10,8},{12,14},{14,12},{16,18},{18,... | collective-permute-start | bytes 393224 | tf_op jit(solution)/shard_map/ppermute | solution.py:406
  53.0 8.7 %collective-permute-start.7 = (f32[256,128]{1,0:T(8,128)S(1)}, f32[256,128]{1,0:T(8,128)S(1)}, u32[]{:S(2)}, u32[]{:S(2)}) collective-permute-start(f32[256,128]{1,0:T(8,128)S(1)} %get-tuple-element.42), channel_id=1, source_target_pairs={{2,5},{3,4},{4,3},{5,2},{6,9},{7,8},{8,7},{9,6},{10,13},{11,12},{1... | collective-permute-start | bytes 393224 | tf_op jit(solution)/shard_map/ppermute | solution.py:405
  66.6 12.8 %collective-permute-start.14 = (f32[1024,128]{1,0:T(8,128)S(1)}, f32[1024,128]{1,0:T(8,128)S(1)}, u32[]{:S(2)}, u32[]{:S(2)}) collective-permute-start(f32[1024,128]{1,0:T(8,128)S(1)} %get-tuple-element.45.refs_0_.refs_2_), channel_id=1, source_target_pairs={{0,2},{2,0},{4,6},{6,4},{8,10},{10,8},{12,14},{14,12},{16,18},{18,... | collective-permute-start | bytes 1572872 | tf_op jit(solution)/shard_map/ppermute | solution.py:404
  66.6 18.9 %collective-permute-start.11 = (f32[1024,128]{1,0:T(8,128)S(1)}, f32[1024,128]{1,0:T(8,128)S(1)}, u32[]{:S(2)}, u32[]{:S(2)}) collective-permute-start(f32[1024,128]{1,0:T(8,128)S(1)} %get-tuple-element.45.refs_0_.refs_2_), channel_id=1, source_target_pairs={{2,4},{4,2},{6,8},{8,6},{10,12},{12,10},{14,16},{16,14},{18,20},{2... | collective-permute-start | bytes 1572872 | tf_op jit(solution)/shard_map/ppermute | solution.py:402
  70.0 4.8 %collective-permute-start.13 = (f32[256,128]{1,0:T(8,128)S(1)}, f32[256,128]{1,0:T(8,128)S(1)}, u32[]{:S(2)}, u32[]{:S(2)}) collective-permute-start(f32[256,128]{1,0:T(8,128)S(1)} %get-tuple-element.46), channel_id=1, source_target_pairs={{0,1},{1,0},{2,3},{3,2},{4,5},{5,4},{6,7},{7,6},{8,9},{9,8},{10,11... | collective-permute-start | bytes 393224 | tf_op jit(solution)/shard_map/ppermute | solution.py:403
  74.8 4.6 %collective-permute-start.15 = (f32[256,128]{1,0:T(8,128)S(1)}, f32[256,128]{1,0:T(8,128)S(1)}, u32[]{:S(2)}, u32[]{:S(2)}) collective-permute-start(f32[256,128]{1,0:T(8,128)S(1)} %collective-permute-done.13.refs_1_), channel_id=1, source_target_pairs={{0,2},{2,0},{4,6},{6,4},{8,10},{10,8},{12,14},{14,12},{16,18},{18,... | collective-permute-start | bytes 393224 | tf_op jit(solution)/shard_map/ppermute | solution.py:406
  76.0 8.7 %collective-permute-start.12 = (f32[256,128]{1,0:T(8,128)S(1)}, f32[256,128]{1,0:T(8,128)S(1)}, u32[]{:S(2)}, u32[]{:S(2)}) collective-permute-start(f32[256,128]{1,0:T(8,128)S(1)} %get-tuple-element.46), channel_id=1, source_target_pairs={{2,5},{3,4},{4,3},{5,2},{6,9},{7,8},{8,7},{9,6},{10,13},{11,12},{1... | collective-permute-start | bytes 393224 | tf_op jit(solution)/shard_map/ppermute | solution.py:405
  89.5 12.6 %collective-permute-start.19 = (f32[1024,128]{1,0:T(8,128)S(1)}, f32[1024,128]{1,0:T(8,128)S(1)}, u32[]{:S(2)}, u32[]{:S(2)}) collective-permute-start(f32[1024,128]{1,0:T(8,128)S(1)} %get-tuple-element.49.refs_0_.refs_2_), channel_id=1, source_target_pairs={{0,2},{2,0},{4,6},{6,4},{8,10},{10,8},{12,14},{14,12},{16,18},{18,... | collective-permute-start | bytes 1572872 | tf_op jit(solution)/shard_map/ppermute | solution.py:404
  89.6 18.9 %collective-permute-start.16 = (f32[1024,128]{1,0:T(8,128)S(1)}, f32[1024,128]{1,0:T(8,128)S(1)}, u32[]{:S(2)}, u32[]{:S(2)}) collective-permute-start(f32[1024,128]{1,0:T(8,128)S(1)} %get-tuple-element.49.refs_0_.refs_2_), channel_id=1, source_target_pairs={{2,4},{4,2},{6,8},{8,6},{10,12},{12,10},{14,16},{16,14},{18,20},{2... | collective-permute-start | bytes 1572872 | tf_op jit(solution)/shard_map/ppermute | solution.py:402
  93.0 4.8 %collective-permute-start.18 = (f32[256,128]{1,0:T(8,128)S(1)}, f32[256,128]{1,0:T(8,128)S(1)}, u32[]{:S(2)}, u32[]{:S(2)}) collective-permute-start(f32[256,128]{1,0:T(8,128)S(1)} %get-tuple-element.50), channel_id=1, source_target_pairs={{0,1},{1,0},{2,3},{3,2},{4,5},{5,4},{6,7},{7,6},{8,9},{9,8},{10,11... | collective-permute-start | bytes 393224 | tf_op jit(solution)/shard_map/ppermute | solution.py:403
  97.7 4.4 %collective-permute-start.20 = (f32[256,128]{1,0:T(8,128)S(1)}, f32[256,128]{1,0:T(8,128)S(1)}, u32[]{:S(2)}, u32[]{:S(2)}) collective-permute-start(f32[256,128]{1,0:T(8,128)S(1)} %collective-permute-done.18.refs_1_), channel_id=1, source_target_pairs={{0,2},{2,0},{4,6},{6,4},{8,10},{10,8},{12,14},{14,12},{16,18},{18,... | collective-permute-start | bytes 393224 | tf_op jit(solution)/shard_map/ppermute | solution.py:406
  98.9 8.7 %collective-permute-start.17 = (f32[256,128]{1,0:T(8,128)S(1)}, f32[256,128]{1,0:T(8,128)S(1)}, u32[]{:S(2)}, u32[]{:S(2)}) collective-permute-start(f32[256,128]{1,0:T(8,128)S(1)} %get-tuple-element.50), channel_id=1, source_target_pairs={{2,5},{3,4},{4,3},{5,2},{6,9},{7,8},{8,7},{9,6},{10,13},{11,12},{1... | collective-permute-start | bytes 393224 | tf_op jit(solution)/shard_map/ppermute | solution.py:405
where the time goes:
time: 114 us; the launch traced here: 113 us
  Pallas kernels  38.4 us (34%)
  starting transfers between devices  38.4 us (34%)
  waiting for transfers between devices  32.6 us (29%)
  local copies, waits for them, and re-layouts  3.61 us (3%)
    pallas_call x9, Pallas kernels, call(): pl.pallas_call(kernel, out_shape=out_shape, in_specs=[SMEM] * len(scalars...  37.6 us
    ppermute x1, waiting for transfers between devices, two_view_plan(): from_beside = lax.ppermute(beside, 'view', swap)  10.8 us
    ppermute x3, waiting for transfers between devices, halo(): side = lax.ppermute(edge, 'view', swap)  10.5 us
    ppermute x3, starting transfers between devices, halo(): outer_z = lax.ppermute(current.array, 'brick', outer)  10 us
    ppermute x3, starting transfers between devices, halo(): outer_side = lax.ppermute(edge, both, diagonal(outer))  9.66 us
    ppermute x1, waiting for transfers between devices, two_view_plan(): from_side = lax.ppermute(across, 'view', swap)  6.29 us
    ppermute x1, starting transfers between devices, two_view_plan(): from_corner = lax.ppermute(corner, both, diagonal(outer))  3.95 us
    ppermute x3, starting transfers between devices, halo(): side = lax.ppermute(edge, 'view', swap)  3.78 us
  transfers between devices with their start and end apart: 21, of which 12 were waited for; matrix products, arithmetic and copies ran while one was open for 0% of the time, Pallas kernels for 19%

commit v1 on v0

--- a/solution.py
+++ b/solution.py
@@ -95,7 +95,7 @@
 
 
 def ratios(seen, blurred):
-    return [jnp.where(b > 0, d / b, 0.0) for d, b in zip(seen, blurred)]
+    return [jnp.where(b > 0, d * pl.reciprocal(b), 0.0) for d, b in zip(seen, blurred)]
 
 
 def gather(total, at, term):
@@ -211,7 +211,8 @@
                 value = wide[:, :width] + wide[:, width:]
                 if views == 2:
                     alone = chosen[1 - v] == 0
-                    power = jnp.where(alone, value, jnp.sqrt(value))
+                    root = jnp.where(value > 0, value * lax.rsqrt(value), value)
+                    power = jnp.where(alone, value, root)
                     power = jnp.where(chosen[v] == 0, 1.0, power)
                     factor = power if factor is None else factor * power
                 else:
@@ -329,10 +330,10 @@
     total = views_data.shape[2]
     window, half = rows + HALO, depth // 2
 
-    def body(place, offsets, estimate, recorded, psf, outer, inner, across, corner, beside):
+    def body(place, estimate, recorded, psf, outer, inner, across, corner, beside):
         mine, theirs = place[1], 1 - place[1]
         edge = pl.multiple_of(jnp.where(mine == 0, rows - HALO, 0), HALO)
-        taps, shifts = small_rows(psf[0], offsets[0, 0], offsets[0, 1], width)
+        taps, shifts = small_rows(psf[0], place[3], place[4], width)
         small = depth * HALO + half * window
         across[pl.ds(small, R), :] = jnp.zeros((R, width), F32)
         across[pl.ds(small, 3), :TAPS] = taps
@@ -369,12 +370,12 @@
     return pl.pallas_call(
         body,
         out_shape=[jax.ShapeDtypeStruct((height, width), F32) for height in heights],
-        in_specs=[SMEM] * 2 + [VMEM] * 3,
+        in_specs=[SMEM] + [VMEM] * 3,
         out_specs=[VMEM] * 5,
         compiler_params=pltpu.CompilerParams(vmem_limit_bytes=10 << 20),
         cost_estimate=pl.CostEstimate(flops=0, bytes_accessed=8 << 20, transcendentals=0),
         name="prepare",
-    )(place, view_offsets, estimate, views_data, psf_taps)
+    )(jnp.concatenate([place, view_offsets[0]]), estimate, views_data, psf_taps)
 
 
 def pair_lists(count):

time: 114 us -> 113 us (level)
    unnamed x9 -> x7, local copies, waits for them, and re-layouts: 3.61 us -> 2.95 us
where the time goes in v1:
time: 113 us
  starting transfers between devices  38.5 us (34%)
  Pallas kernels  38 us (34%)
  waiting for transfers between devices  32.4 us (29%)
  local copies, waits for them, and re-layouts  2.95 us (3%)
    pallas_call x9, Pallas kernels, call(): pl.pallas_call(kernel, out_shape=out_shape, in_specs=[SMEM] * len(scalars...  37.2 us
    ppermute x1, waiting for transfers between devices, two_view_plan(): from_beside = lax.ppermute(beside, 'view', swap)  10.7 us
    ppermute x3, waiting for transfers between devices, halo(): side = lax.ppermute(edge, 'view', swap)  10.4 us
    ppermute x3, starting transfers between devices, halo(): outer_z = lax.ppermute(current.array, 'brick', outer)  10.1 us
    ppermute x3, starting transfers between devices, halo(): outer_side = lax.ppermute(edge, both, diagonal(outer))  9.67 us
    ppermute x1, waiting for transfers between devices, two_view_plan(): from_side = lax.ppermute(across, 'view', swap)  6.29 us
    ppermute x1, starting transfers between devices, two_view_plan(): from_corner = lax.ppermute(corner, both, diagonal(outer))  3.95 us
    ppermute x3, starting transfers between devices, halo(): side = lax.ppermute(edge, 'view', swap)  3.8 us
  transfers between devices with their start and end apart: 21, of which 12 were waited for; matrix products, arithmetic and copies ran while one was open for 0% of the time, Pallas kernels for 19%

profile of v1, /device:TPU:17, one launch (start us, length us, event | category | flops | bytes accessed | tf_op | source)
XLA Modules:
  0.0 112.9 jit_solution(15385571242356639677)
XLA Ops:
  0.0 0.7 copy.6.psf
  0.7 0.7 pad_add_fusion.1.place
  1.4 1.2 %copy-done = f32[1,16,128,128]{3,2,1,0:T(8,128)S(1)} copy-done((f32[1,16,128,128]{3,2,1,0:T(8,128)S(1)}, f32[1,16,128,128]{3,2,1,0:T(8,128)}, u32[]{:S(2)}) %copy-start) | copy-done | bytes 1048600
  2.6 1.0 copy-done.1
  3.7 0.7 prepare.1
  4.4 1.3 %collective-permute-start.2 = (f32[904,128]{1,0:T(8,128)S(1)}, f32[904,128]{1,0:T(8,128)S(1)}, u32[]{:S(2)}, u32[]{:S(2)}) collective-permute-start(f32[904,128]{1,0:T(8,128)S(1)} %get-tuple-element.32.refs_1_), channel_id=1, source_target_pairs={{0,1},{1,0},{2,3},{3,2},{4,5},{5,4},{6,7},{7,6},{8,9},{9,8},{10,11... | collective-permute-start | bytes 1388552 | tf_op jit(solution)/shard_map/ppermute | solution.py:417
  5.7 1.0 collective-permute-start.3
  6.7 3.0 %collective-permute-start = (f32[1664,128]{1,0:T(8,128)S(1)}, f32[1664,128]{1,0:T(8,128)S(1)}, u32[]{:S(2)}, u32[]{:S(2)}) collective-permute-start(f32[1664,128]{1,0:T(8,128)S(1)} %get-tuple-element.30.refs_12_.refs_14_), channel_id=1, source_target_pairs={{2,4},{4,2},{6,8},{8,6},{10,12},{12,10},{14,16},{16,14},{18,20},{2... | collective-permute-start | bytes 2555912 | tf_op jit(solution)/shard_map/ppermute | solution.py:416
  9.7 6.3 %collective-permute-done.2.refs_2_.refs_1_.refs_8_ = f32[904,128]{1,0:T(8,128)S(1)} collective-permute-done((f32[904,128]{1,0:T(8,128)S(1)}, f32[904,128]{1,0:T(8,128)S(1)}, u32[]{:S(2)}, u32[]{:S(2)}) %collective-permute-start.2) | collective-permute-done | bytes 462880 | tf_op jit(solution)/shard_map/ppermute | solution.py:417
  16.0 1.5 %collective-permute-start.4 = (f32[904,128]{1,0:T(8,128)S(1)}, f32[904,128]{1,0:T(8,128)S(1)}, u32[]{:S(2)}, u32[]{:S(2)}) collective-permute-start(f32[904,128]{1,0:T(8,128)S(1)} %collective-permute-done.2.refs_2_.refs_1_.refs_8_), channel_id=1, source_target_pairs={{0,2},{2,0},{4,6},{6,4},{8,10},{10,8},{12,14},{14,12},{16,18},{18,... | collective-permute-start | bytes 1388552 | tf_op jit(solution)/shard_map/ppermute | solution.py:421
  17.5 4.0 %collective-permute-start.1 = (f32[896,128]{1,0:T(8,128)S(1)}, f32[896,128]{1,0:T(8,128)S(1)}, u32[]{:S(2)}, u32[]{:S(2)}) collective-permute-start(f32[896,128]{1,0:T(8,128)S(1)} %get-tuple-element.31), channel_id=1, source_target_pairs={{2,5},{3,4},{4,3},{5,2},{6,9},{7,8},{8,7},{9,6},{10,13},{11,12},{1... | collective-permute-start | bytes 1376264 | tf_op jit(solution)/shard_map/ppermute | solution.py:419
  21.5 0.3 collective-permute-start.5
  21.8 0.1 pad_add_fusion.refs_0_
  21.9 2.2 %shard_map.55 = (f32[2,17,8,128]{3,2,1,0:T(8,128)S(1)}, bf16[160,240]{1,0:T(8,128)(2,1)S(1)}, bf16[2,256,256]{2,1,0:T(8,128)(2,1)S(1)}, bf16[2,64,240]{2,1,0:T(8,128)(2,1)S(1)}, bf16[2,256,256]{2,1,0:T(8,128)(2,1)S(1)}) custom-call(s32[3]{0:T(128)S(1)} %pad_add_fusion.refs_0_, f32[904,128]{1,0:T(8,128)S(1)} %get-tuple-element.32.refs_1_, ...), custom_call_target="tpu_custom_call" | custom-call | flops 200000000 | bytes 1048576 | tf_op jit(solution)/shard_map/pallas_call | solution.py:63
  24.1 4.7 %shard_map.56 = (f32[2,16,80,128]{3,2,1,0:T(8,128)S(1)}, f32[2,16,80,128]{3,2,1,0:T(8,128)S(1)}) custom-call(f32[1664,128]{1,0:T(8,128)S(1)} %get-tuple-element.29.refs_0_.refs_2_.refs_7_, f32[904,128]{1,0:T(8,128)S(1)} %collective-permute-done.2.refs_2_.refs_1_.refs_8_, f32[1664,128]{1,0:T(8,128)S(1)} %collective-permute-done.3.refs_2_.refs_9_, ...), custom_call_target="tpu_custom_call" | custom-call | flops 2000000000 | bytes 1048576 | tf_op jit(solution)/shard_map/pallas_call | solution.py:63
  28.9 10.7 %collective-permute-done.5.refs_13_.refs_15_ = f32[640,128]{1,0:T(8,128)S(1)} collective-permute-done((f32[640,128]{1,0:T(8,128)S(1)}, f32[640,128]{1,0:T(8,128)S(1)}, u32[]{:S(2)}, u32[]{:S(2)}) %collective-permute-start.5) | collective-permute-done | bytes 327712 | tf_op jit(solution)/shard_map/ppermute | solution.py:420
  39.6 0.1 collective-permute-done.refs_3_.refs_12_
  39.6 3.8 %shard_map.57 = (f32[1024,128]{1,0:T(8,128)S(1)}, f32[256,128]{1,0:T(8,128)S(1)}) custom-call(s32[3]{0:T(128)S(1)} %pad_add_fusion.refs_0_, s32[1,2]{1,0:T(1,128)S(1)} %copy-done.2, f32[1664,128]{1,0:T(8,128)S(1)} %get-tuple-element.29.refs_0_.refs_2_.refs_7_, f32[1664,128]{1,0:T(8,128)S(1)} %collective-permute-done.refs_3_.refs_12_, ...), custom_call_target="tpu_custom_call" | custom-call | flops 2000000000 | bytes 1048576 | tf_op jit(solution)/shard_map/pallas_call | solution.py:63
  43.5 0.1 collective-permute-start.9
  43.6 3.4 %collective-permute-start.6 = (f32[1024,128]{1,0:T(8,128)S(1)}, f32[1024,128]{1,0:T(8,128)S(1)}, u32[]{:S(2)}, u32[]{:S(2)}) collective-permute-start(f32[1024,128]{1,0:T(8,128)S(1)} %get-tuple-element.41.refs_0_.refs_2_), channel_id=1, source_target_pairs={{2,4},{4,2},{6,8},{8,6},{10,12},{12,10},{14,16},{16,14},{18,20},{2... | collective-permute-start | bytes 1572872 | tf_op jit(solution)/shard_map/ppermute | solution.py:403
  46.9 1.3 %collective-permute-start.8 = (f32[256,128]{1,0:T(8,128)S(1)}, f32[256,128]{1,0:T(8,128)S(1)}, u32[]{:S(2)}, u32[]{:S(2)}) collective-permute-start(f32[256,128]{1,0:T(8,128)S(1)} %get-tuple-element.42), channel_id=1, source_target_pairs={{0,1},{1,0},{2,3},{3,2},{4,5},{5,4},{6,7},{7,6},{8,9},{9,8},{10,11... | collective-permute-start | bytes 393224 | tf_op jit(solution)/shard_map/ppermute | solution.py:404
  48.2 3.5 %collective-permute-done.8.refs_1_ = f32[256,128]{1,0:T(8,128)S(1)} collective-permute-done((f32[256,128]{1,0:T(8,128)S(1)}, f32[256,128]{1,0:T(8,128)S(1)}, u32[]{:S(2)}, u32[]{:S(2)}) %collective-permute-start.8) | collective-permute-done | bytes 131104 | tf_op jit(solution)/shard_map/ppermute | solution.py:404
  51.7 1.2 %collective-permute-start.10 = (f32[256,128]{1,0:T(8,128)S(1)}, f32[256,128]{1,0:T(8,128)S(1)}, u32[]{:S(2)}, u32[]{:S(2)}) collective-permute-start(f32[256,128]{1,0:T(8,128)S(1)} %collective-permute-done.8.refs_1_), channel_id=1, source_target_pairs={{0,2},{2,0},{4,6},{6,4},{8,10},{10,8},{12,14},{14,12},{16,18},{18,... | collective-permute-start | bytes 393224 | tf_op jit(solution)/shard_map/ppermute | solution.py:407
  52.9 3.2 %collective-permute-start.7 = (f32[256,128]{1,0:T(8,128)S(1)}, f32[256,128]{1,0:T(8,128)S(1)}, u32[]{:S(2)}, u32[]{:S(2)}) collective-permute-start(f32[256,128]{1,0:T(8,128)S(1)} %get-tuple-element.42), channel_id=1, source_target_pairs={{2,5},{3,4},{4,3},{5,2},{6,9},{7,8},{8,7},{9,6},{10,13},{11,12},{1... | collective-permute-start | bytes 393224 | tf_op jit(solution)/shard_map/ppermute | solution.py:406
  56.1 4.7 %shard_map.58 = (f32[2,16,80,128]{3,2,1,0:T(8,128)S(1)}, f32[2,16,80,128]{3,2,1,0:T(8,128)S(1)}) custom-call(f32[1024,128]{1,0:T(8,128)S(1)} %get-tuple-element.41.refs_0_.refs_2_, f32[256,128]{1,0:T(8,128)S(1)} %collective-permute-done.8.refs_1_, f32[1024,128]{1,0:T(8,128)S(1)} %collective-permute-done.9.refs_2_, ...), custom_call_target="tpu_custom_call" | custom-call | flops 2000000000 | bytes 1048576 | tf_op jit(solution)/shard_map/pallas_call | solution.py:63
  60.8 0.8 collective-permute-done.7.refs_4_
  61.6 0.9 collective-permute-done.6.refs_3_
  62.5 3.8 %shard_map.59 = (f32[1024,128]{1,0:T(8,128)S(1)}, f32[256,128]{1,0:T(8,128)S(1)}) custom-call(s32[3]{0:T(128)S(1)} %pad_add_fusion.refs_0_, s32[1,2]{1,0:T(1,128)S(1)} %copy-done.2, f32[1024,128]{1,0:T(8,128)S(1)} %get-tuple-element.41.refs_0_.refs_2_, f32[1024,128]{1,0:T(8,128)S(1)} %collective-permute-done.6.refs_3_, ...), custom_call_target="tpu_custom_call" | custom-call | flops 2000000000 | bytes 1048576 | tf_op jit(solution)/shard_map/pallas_call | solution.py:63
  66.3 0.1 collective-permute-start.14
  66.4 3.4 %collective-permute-start.11 = (f32[1024,128]{1,0:T(8,128)S(1)}, f32[1024,128]{1,0:T(8,128)S(1)}, u32[]{:S(2)}, u32[]{:S(2)}) collective-permute-start(f32[1024,128]{1,0:T(8,128)S(1)} %get-tuple-element.45.refs_0_.refs_2_), channel_id=1, source_target_pairs={{2,4},{4,2},{6,8},{8,6},{10,12},{12,10},{14,16},{16,14},{18,20},{2... | collective-permute-start | bytes 1572872 | tf_op jit(solution)/shard_map/ppermute | solution.py:403
  69.8 1.3 %collective-permute-start.13 = (f32[256,128]{1,0:T(8,128)S(1)}, f32[256,128]{1,0:T(8,128)S(1)}, u32[]{:S(2)}, u32[]{:S(2)}) collective-permute-start(f32[256,128]{1,0:T(8,128)S(1)} %get-tuple-element.46), channel_id=1, source_target_pairs={{0,1},{1,0},{2,3},{3,2},{4,5},{5,4},{6,7},{7,6},{8,9},{9,8},{10,11... | collective-permute-start | bytes 393224 | tf_op jit(solution)/shard_map/ppermute | solution.py:404
  71.0 3.5 %collective-permute-done.13.refs_1_ = f32[256,128]{1,0:T(8,128)S(1)} collective-permute-done((f32[256,128]{1,0:T(8,128)S(1)}, f32[256,128]{1,0:T(8,128)S(1)}, u32[]{:S(2)}, u32[]{:S(2)}) %collective-permute-start.13) | collective-permute-done | bytes 131104 | tf_op jit(solution)/shard_map/ppermute | solution.py:404
  74.5 1.2 %collective-permute-start.15 = (f32[256,128]{1,0:T(8,128)S(1)}, f32[256,128]{1,0:T(8,128)S(1)}, u32[]{:S(2)}, u32[]{:S(2)}) collective-permute-start(f32[256,128]{1,0:T(8,128)S(1)} %collective-permute-done.13.refs_1_), channel_id=1, source_target_pairs={{0,2},{2,0},{4,6},{6,4},{8,10},{10,8},{12,14},{14,12},{16,18},{18,... | collective-permute-start | bytes 393224 | tf_op jit(solution)/shard_map/ppermute | solution.py:407
  75.8 3.3 %collective-permute-start.12 = (f32[256,128]{1,0:T(8,128)S(1)}, f32[256,128]{1,0:T(8,128)S(1)}, u32[]{:S(2)}, u32[]{:S(2)}) collective-permute-start(f32[256,128]{1,0:T(8,128)S(1)} %get-tuple-element.46), channel_id=1, source_target_pairs={{2,5},{3,4},{4,3},{5,2},{6,9},{7,8},{8,7},{9,6},{10,13},{11,12},{1... | collective-permute-start | bytes 393224 | tf_op jit(solution)/shard_map/ppermute | solution.py:406
  79.1 4.7 %shard_map.60 = (f32[2,16,80,128]{3,2,1,0:T(8,128)S(1)}, f32[2,16,80,128]{3,2,1,0:T(8,128)S(1)}) custom-call(f32[1024,128]{1,0:T(8,128)S(1)} %get-tuple-element.45.refs_0_.refs_2_, f32[256,128]{1,0:T(8,128)S(1)} %collective-permute-done.13.refs_1_, f32[1024,128]{1,0:T(8,128)S(1)} %collective-permute-done.14.refs_2_, ...), custom_call_target="tpu_custom_call" | custom-call | flops 2000000000 | bytes 1048576 | tf_op jit(solution)/shard_map/pallas_call | solution.py:63
  83.8 0.6 collective-permute-done.12.refs_4_
  84.4 0.9 collective-permute-done.11.refs_3_
  85.3 3.9 %shard_map.61 = (f32[1024,128]{1,0:T(8,128)S(1)}, f32[256,128]{1,0:T(8,128)S(1)}) custom-call(s32[3]{0:T(128)S(1)} %pad_add_fusion.refs_0_, s32[1,2]{1,0:T(1,128)S(1)} %copy-done.2, f32[1024,128]{1,0:T(8,128)S(1)} %get-tuple-element.45.refs_0_.refs_2_, f32[1024,128]{1,0:T(8,128)S(1)} %collective-permute-done.11.refs_3_, ...), custom_call_target="tpu_custom_call" | custom-call | flops 2000000000 | bytes 1048576 | tf_op jit(solution)/shard_map/pallas_call | solution.py:63
  89.2 0.1 collective-permute-start.19
  89.3 3.4 %collective-permute-start.16 = (f32[1024,128]{1,0:T(8,128)S(1)}, f32[1024,128]{1,0:T(8,128)S(1)}, u32[]{:S(2)}, u32[]{:S(2)}) collective-permute-start(f32[1024,128]{1,0:T(8,128)S(1)} %get-tuple-element.49.refs_0_.refs_2_), channel_id=1, source_target_pairs={{2,4},{4,2},{6,8},{8,6},{10,12},{12,10},{14,16},{16,14},{18,20},{2... | collective-permute-start | bytes 1572872 | tf_op jit(solution)/shard_map/ppermute | solution.py:403
  92.6 1.3 %collective-permute-start.18 = (f32[256,128]{1,0:T(8,128)S(1)}, f32[256,128]{1,0:T(8,128)S(1)}, u32[]{:S(2)}, u32[]{:S(2)}) collective-permute-start(f32[256,128]{1,0:T(8,128)S(1)} %get-tuple-element.50), channel_id=1, source_target_pairs={{0,1},{1,0},{2,3},{3,2},{4,5},{5,4},{6,7},{7,6},{8,9},{9,8},{10,11... | collective-permute-start | bytes 393224 | tf_op jit(solution)/shard_map/ppermute | solution.py:404
  93.9 3.5 %collective-permute-done.18.refs_1_ = f32[256,128]{1,0:T(8,128)S(1)} collective-permute-done((f32[256,128]{1,0:T(8,128)S(1)}, f32[256,128]{1,0:T(8,128)S(1)}, u32[]{:S(2)}, u32[]{:S(2)}) %collective-permute-start.18) | collective-permute-done | bytes 131104 | tf_op jit(solution)/shard_map/ppermute | solution.py:404
  97.4 1.2 %collective-permute-start.20 = (f32[256,128]{1,0:T(8,128)S(1)}, f32[256,128]{1,0:T(8,128)S(1)}, u32[]{:S(2)}, u32[]{:S(2)}) collective-permute-start(f32[256,128]{1,0:T(8,128)S(1)} %collective-permute-done.18.refs_1_), channel_id=1, source_target_pairs={{0,2},{2,0},{4,6},{6,4},{8,10},{10,8},{12,14},{14,12},{16,18},{18,... | collective-permute-start | bytes 393224 | tf_op jit(solution)/shard_map/ppermute | solution.py:407
  98.6 3.2 %collective-permute-start.17 = (f32[256,128]{1,0:T(8,128)S(1)}, f32[256,128]{1,0:T(8,128)S(1)}, u32[]{:S(2)}, u32[]{:S(2)}) collective-permute-start(f32[256,128]{1,0:T(8,128)S(1)} %get-tuple-element.50), channel_id=1, source_target_pairs={{2,5},{3,4},{4,3},{5,2},{6,9},{7,8},{8,7},{9,6},{10,13},{11,12},{1... | collective-permute-start | bytes 393224 | tf_op jit(solution)/shard_map/ppermute | solution.py:406
  101.8 4.7 %shard_map.62 = (f32[2,16,80,128]{3,2,1,0:T(8,128)S(1)}, f32[2,16,80,128]{3,2,1,0:T(8,128)S(1)}) custom-call(f32[1024,128]{1,0:T(8,128)S(1)} %get-tuple-element.49.refs_0_.refs_2_, f32[256,128]{1,0:T(8,128)S(1)} %collective-permute-done.18.refs_1_, f32[1024,128]{1,0:T(8,128)S(1)} %collective-permute-done.19.refs_2_, ...), custom_call_target="tpu_custom_call" | custom-call | flops 2000000000 | bytes 1048576 | tf_op jit(solution)/shard_map/pallas_call | solution.py:63
  106.5 0.8 collective-permute-done.17.refs_4_
  107.3 0.9 collective-permute-done.16.refs_3_
  108.2 4.6 %shard_map.63 = f32[16,64,128]{2,1,0:T(8,128)} custom-call(s32[3]{0:T(128)S(1)} %pad_add_fusion.refs_0_, s32[1,2]{1,0:T(1,128)S(1)} %copy-done.2, f32[1024,128]{1,0:T(8,128)S(1)} %get-tuple-element.49.refs_0_.refs_2_, f32[1024,128]{1,0:T(8,128)S(1)} %collective-permute-done.16.refs_3_, f32[256,128]{1,0:T(8,128)S(1)} %collective-permute-done.17.refs_4_, ...), custom_call_target="tpu_custom_call" | custom-call | flops 2000000000 | bytes 1048576 | tf_op jit(solution)/shard_map/pallas_call | solution.py:63
  (13 shorter events, 0.0 us)
Async XLA Ops:
  1.4 1.2 %copy-start = (f32[1,16,128,128]{3,2,1,0:T(8,128)S(1)}, f32[1,16,128,128]{3,2,1,0:T(8,128)}, u32[]{:S(2)}) copy-start(f32[1,16,128,128]{3,2,1,0:T(8,128)} %recorded.1) | copy-start | bytes 3145732
  2.6 1.0 copy-start.1
  4.4 11.6 %collective-permute-start.2 = (f32[904,128]{1,0:T(8,128)S(1)}, f32[904,128]{1,0:T(8,128)S(1)}, u32[]{:S(2)}, u32[]{:S(2)}) collective-permute-start(f32[904,128]{1,0:T(8,128)S(1)} %get-tuple-element.32.refs_1_), channel_id=1, source_target_pairs={{0,1},{1,0},{2,3},{3,2},{4,5},{5,4},{6,7},{7,6},{8,9},{9,8},{10,11... | collective-permute-start | bytes 1388552 | tf_op jit(solution)/shard_map/ppermute | solution.py:417
  5.7 18.4 %collective-permute-start.3 = (f32[1664,128]{1,0:T(8,128)S(1)}, f32[1664,128]{1,0:T(8,128)S(1)}, u32[]{:S(2)}, u32[]{:S(2)}) collective-permute-start(f32[1664,128]{1,0:T(8,128)S(1)} %get-tuple-element.29.refs_0_.refs_2_.refs_7_), channel_id=1, source_target_pairs={{0,2},{2,0},{4,6},{6,4},{8,10},{10,8},{12,14},{14,12},{16,18},{18,... | collective-permute-start | bytes 2555912 | tf_op jit(solution)/shard_map/ppermute | solution.py:418
  6.7 33.0 %collective-permute-start = (f32[1664,128]{1,0:T(8,128)S(1)}, f32[1664,128]{1,0:T(8,128)S(1)}, u32[]{:S(2)}, u32[]{:S(2)}) collective-permute-start(f32[1664,128]{1,0:T(8,128)S(1)} %get-tuple-element.30.refs_12_.refs_14_), channel_id=1, source_target_pairs={{2,4},{4,2},{6,8},{8,6},{10,12},{12,10},{14,16},{16,14},{18,20},{2... | collective-permute-start | bytes 2555912 | tf_op jit(solution)/shard_map/ppermute | solution.py:416
  16.0 8.1 %collective-permute-start.4 = (f32[904,128]{1,0:T(8,128)S(1)}, f32[904,128]{1,0:T(8,128)S(1)}, u32[]{:S(2)}, u32[]{:S(2)}) collective-permute-start(f32[904,128]{1,0:T(8,128)S(1)} %collective-permute-done.2.refs_2_.refs_1_.refs_8_), channel_id=1, source_target_pairs={{0,2},{2,0},{4,6},{6,4},{8,10},{10,8},{12,14},{14,12},{16,18},{18,... | collective-permute-start | bytes 1388552 | tf_op jit(solution)/shard_map/ppermute | solution.py:421
  17.5 22.0 %collective-permute-start.1 = (f32[896,128]{1,0:T(8,128)S(1)}, f32[896,128]{1,0:T(8,128)S(1)}, u32[]{:S(2)}, u32[]{:S(2)}) collective-permute-start(f32[896,128]{1,0:T(8,128)S(1)} %get-tuple-element.31), channel_id=1, source_target_pairs={{2,5},{3,4},{4,3},{5,2},{6,9},{7,8},{8,7},{9,6},{10,13},{11,12},{1... | collective-permute-start | bytes 1376264 | tf_op jit(solution)/shard_map/ppermute | solution.py:419
  21.5 18.1 %collective-permute-start.5 = (f32[640,128]{1,0:T(8,128)S(1)}, f32[640,128]{1,0:T(8,128)S(1)}, u32[]{:S(2)}, u32[]{:S(2)}) collective-permute-start(f32[640,128]{1,0:T(8,128)S(1)} %get-tuple-element.40), channel_id=1, source_target_pairs={{0,1},{1,0},{2,3},{3,2},{4,5},{5,4},{6,7},{7,6},{8,9},{9,8},{10,11... | collective-permute-start | bytes 983048 | tf_op jit(solution)/shard_map/ppermute | solution.py:420
  24.1 15.5 %copy-start.2 = (s32[1,2]{1,0:T(1,128)S(1)}, s32[1,2]{1,0:T(1,128)}, u32[]{:S(2)}) copy-start(s32[1,2]{1,0:T(1,128)} %refs_1_.7) | copy-start | bytes 28
  43.5 12.6 %collective-permute-start.9 = (f32[1024,128]{1,0:T(8,128)S(1)}, f32[1024,128]{1,0:T(8,128)S(1)}, u32[]{:S(2)}, u32[]{:S(2)}) collective-permute-start(f32[1024,128]{1,0:T(8,128)S(1)} %get-tuple-element.41.refs_0_.refs_2_), channel_id=1, source_target_pairs={{0,2},{2,0},{4,6},{6,4},{8,10},{10,8},{12,14},{14,12},{16,18},{18,... | collective-permute-start | bytes 1572872 | tf_op jit(solution)/shard_map/ppermute | solution.py:405
  43.6 18.9 %collective-permute-start.6 = (f32[1024,128]{1,0:T(8,128)S(1)}, f32[1024,128]{1,0:T(8,128)S(1)}, u32[]{:S(2)}, u32[]{:S(2)}) collective-permute-start(f32[1024,128]{1,0:T(8,128)S(1)} %get-tuple-element.41.refs_0_.refs_2_), channel_id=1, source_target_pairs={{2,4},{4,2},{6,8},{8,6},{10,12},{12,10},{14,16},{16,14},{18,20},{2... | collective-permute-start | bytes 1572872 | tf_op jit(solution)/shard_map/ppermute | solution.py:403
  46.9 4.7 %collective-permute-start.8 = (f32[256,128]{1,0:T(8,128)S(1)}, f32[256,128]{1,0:T(8,128)S(1)}, u32[]{:S(2)}, u32[]{:S(2)}) collective-permute-start(f32[256,128]{1,0:T(8,128)S(1)} %get-tuple-element.42), channel_id=1, source_target_pairs={{0,1},{1,0},{2,3},{3,2},{4,5},{5,4},{6,7},{7,6},{8,9},{9,8},{10,11... | collective-permute-start | bytes 393224 | tf_op jit(solution)/shard_map/ppermute | solution.py:404
  51.7 4.4 %collective-permute-start.10 = (f32[256,128]{1,0:T(8,128)S(1)}, f32[256,128]{1,0:T(8,128)S(1)}, u32[]{:S(2)}, u32[]{:S(2)}) collective-permute-start(f32[256,128]{1,0:T(8,128)S(1)} %collective-permute-done.8.refs_1_), channel_id=1, source_target_pairs={{0,2},{2,0},{4,6},{6,4},{8,10},{10,8},{12,14},{14,12},{16,18},{18,... | collective-permute-start | bytes 393224 | tf_op jit(solution)/shard_map/ppermute | solution.py:407
  52.9 8.7 %collective-permute-start.7 = (f32[256,128]{1,0:T(8,128)S(1)}, f32[256,128]{1,0:T(8,128)S(1)}, u32[]{:S(2)}, u32[]{:S(2)}) collective-permute-start(f32[256,128]{1,0:T(8,128)S(1)} %get-tuple-element.42), channel_id=1, source_target_pairs={{2,5},{3,4},{4,3},{5,2},{6,9},{7,8},{8,7},{9,6},{10,13},{11,12},{1... | collective-permute-start | bytes 393224 | tf_op jit(solution)/shard_map/ppermute | solution.py:406
  66.3 12.8 %collective-permute-start.14 = (f32[1024,128]{1,0:T(8,128)S(1)}, f32[1024,128]{1,0:T(8,128)S(1)}, u32[]{:S(2)}, u32[]{:S(2)}) collective-permute-start(f32[1024,128]{1,0:T(8,128)S(1)} %get-tuple-element.45.refs_0_.refs_2_), channel_id=1, source_target_pairs={{0,2},{2,0},{4,6},{6,4},{8,10},{10,8},{12,14},{14,12},{16,18},{18,... | collective-permute-start | bytes 1572872 | tf_op jit(solution)/shard_map/ppermute | solution.py:405
  66.4 18.9 %collective-permute-start.11 = (f32[1024,128]{1,0:T(8,128)S(1)}, f32[1024,128]{1,0:T(8,128)S(1)}, u32[]{:S(2)}, u32[]{:S(2)}) collective-permute-start(f32[1024,128]{1,0:T(8,128)S(1)} %get-tuple-element.45.refs_0_.refs_2_), channel_id=1, source_target_pairs={{2,4},{4,2},{6,8},{8,6},{10,12},{12,10},{14,16},{16,14},{18,20},{2... | collective-permute-start | bytes 1572872 | tf_op jit(solution)/shard_map/ppermute | solution.py:403
  69.8 4.7 %collective-permute-start.13 = (f32[256,128]{1,0:T(8,128)S(1)}, f32[256,128]{1,0:T(8,128)S(1)}, u32[]{:S(2)}, u32[]{:S(2)}) collective-permute-start(f32[256,128]{1,0:T(8,128)S(1)} %get-tuple-element.46), channel_id=1, source_target_pairs={{0,1},{1,0},{2,3},{3,2},{4,5},{5,4},{6,7},{7,6},{8,9},{9,8},{10,11... | collective-permute-start | bytes 393224 | tf_op jit(solution)/shard_map/ppermute | solution.py:404
  74.5 4.6 %collective-permute-start.15 = (f32[256,128]{1,0:T(8,128)S(1)}, f32[256,128]{1,0:T(8,128)S(1)}, u32[]{:S(2)}, u32[]{:S(2)}) collective-permute-start(f32[256,128]{1,0:T(8,128)S(1)} %collective-permute-done.13.refs_1_), channel_id=1, source_target_pairs={{0,2},{2,0},{4,6},{6,4},{8,10},{10,8},{12,14},{14,12},{16,18},{18,... | collective-permute-start | bytes 393224 | tf_op jit(solution)/shard_map/ppermute | solution.py:407
  75.8 8.7 %collective-permute-start.12 = (f32[256,128]{1,0:T(8,128)S(1)}, f32[256,128]{1,0:T(8,128)S(1)}, u32[]{:S(2)}, u32[]{:S(2)}) collective-permute-start(f32[256,128]{1,0:T(8,128)S(1)} %get-tuple-element.46), channel_id=1, source_target_pairs={{2,5},{3,4},{4,3},{5,2},{6,9},{7,8},{8,7},{9,6},{10,13},{11,12},{1... | collective-permute-start | bytes 393224 | tf_op jit(solution)/shard_map/ppermute | solution.py:406
  89.2 12.6 %collective-permute-start.19 = (f32[1024,128]{1,0:T(8,128)S(1)}, f32[1024,128]{1,0:T(8,128)S(1)}, u32[]{:S(2)}, u32[]{:S(2)}) collective-permute-start(f32[1024,128]{1,0:T(8,128)S(1)} %get-tuple-element.49.refs_0_.refs_2_), channel_id=1, source_target_pairs={{0,2},{2,0},{4,6},{6,4},{8,10},{10,8},{12,14},{14,12},{16,18},{18,... | collective-permute-start | bytes 1572872 | tf_op jit(solution)/shard_map/ppermute | solution.py:405
  89.3 18.9 %collective-permute-start.16 = (f32[1024,128]{1,0:T(8,128)S(1)}, f32[1024,128]{1,0:T(8,128)S(1)}, u32[]{:S(2)}, u32[]{:S(2)}) collective-permute-start(f32[1024,128]{1,0:T(8,128)S(1)} %get-tuple-element.49.refs_0_.refs_2_), channel_id=1, source_target_pairs={{2,4},{4,2},{6,8},{8,6},{10,12},{12,10},{14,16},{16,14},{18,20},{2... | collective-permute-start | bytes 1572872 | tf_op jit(solution)/shard_map/ppermute | solution.py:403
  92.6 4.7 %collective-permute-start.18 = (f32[256,128]{1,0:T(8,128)S(1)}, f32[256,128]{1,0:T(8,128)S(1)}, u32[]{:S(2)}, u32[]{:S(2)}) collective-permute-start(f32[256,128]{1,0:T(8,128)S(1)} %get-tuple-element.50), channel_id=1, source_target_pairs={{0,1},{1,0},{2,3},{3,2},{4,5},{5,4},{6,7},{7,6},{8,9},{9,8},{10,11... | collective-permute-start | bytes 393224 | tf_op jit(solution)/shard_map/ppermute | solution.py:404
  97.4 4.4 %collective-permute-start.20 = (f32[256,128]{1,0:T(8,128)S(1)}, f32[256,128]{1,0:T(8,128)S(1)}, u32[]{:S(2)}, u32[]{:S(2)}) collective-permute-start(f32[256,128]{1,0:T(8,128)S(1)} %collective-permute-done.18.refs_1_), channel_id=1, source_target_pairs={{0,2},{2,0},{4,6},{6,4},{8,10},{10,8},{12,14},{14,12},{16,18},{18,... | collective-permute-start | bytes 393224 | tf_op jit(solution)/shard_map/ppermute | solution.py:407
  98.6 8.7 %collective-permute-start.17 = (f32[256,128]{1,0:T(8,128)S(1)}, f32[256,128]{1,0:T(8,128)S(1)}, u32[]{:S(2)}, u32[]{:S(2)}) collective-permute-start(f32[256,128]{1,0:T(8,128)S(1)} %get-tuple-element.50), channel_id=1, source_target_pairs={{2,5},{3,4},{4,3},{5,2},{6,9},{7,8},{8,7},{9,6},{10,13},{11,12},{1... | collective-permute-start | bytes 393224 | tf_op jit(solution)/shard_map/ppermute | solution.py:406
